TPU v7x, 512 devices: a whole 4x8x8 slice. The times are simulated.
512 devices in a mesh: row: 16 (over x_hi, y), col: 32 (over z, x_lo, core).
Axes of the slice: x: 4 (x_hi: 2, x_lo: 2; x = x_hi * 2 + x_lo), y: 8, z: 8, core: 2. Of those that a mesh axis runs over, the one named last changes fastest.
Arguments:
- base_input: bfloat16 [1024, 16384], P('col', 'row'), may hold values from -6 to 6
- layer_input: bfloat16 [1024, 16384], P('row', 'col'), may hold values from -6 to 6
- out_grad: bfloat16 [1024, 16384], P('col', 'row'), may hold values from -6 to 6
- cross_weight: bfloat16 [16384, 16384], P('row', 'col'), may hold values from -0.046875 to 0.046875
- cross_bias: bfloat16 [16384], P('row'), may hold values from -5 to 5
Outputs:
- weight_grad: float32 [16384, 16384], P('row', 'col')
- bias_grad: float32 [16384], P('row')
- base_grad: bfloat16 [1024, 16384], P('col', 'row')
- branch_grad: bfloat16 [1024, 16384], P('row', 'col')
All inputs are finite; a program needn't handle non-finite values.
Results may differ from a plain program's by a relative error of at most 0.019.
Values may be sent and summed in bfloat16 or wider, within the bound.
A program may use at most 64 MiB of HBM per device.

v0:
```python
import jax
import jax.numpy as jnp
from jax import lax
from jax.sharding import PartitionSpec as P


def on_device(base_input, layer_input, out_grad, cross_weight, cross_bias):
    input_panel = lax.all_gather(layer_input, "row", axis=0, tiled=True)
    grad_panel, base_panel = (
        lax.all_gather(out_grad, "col", axis=0, tiled=True),
        lax.all_gather(base_input, "col", axis=0, tiled=True),
    )
    hidden_panel = (grad_panel.astype(jnp.float32) * base_panel.astype(jnp.float32)).astype(
        jnp.bfloat16
    )
    weight_grad = lax.dot_general(
        hidden_panel, input_panel, (((0,), (0,)), ((), ())), preferred_element_type=jnp.float32
    )
    bias_grad = jnp.sum(hidden_panel, axis=0, dtype=jnp.float32)
    rows = input_panel
    preact = lax.psum_scatter(
        lax.dot_general(
            rows, cross_weight, (((1,), (1,)), ((), ())), preferred_element_type=jnp.float32
        ).astype(jnp.bfloat16),
        "col",
        scatter_dimension=0,
        tiled=True,
    ).astype(jnp.float32)
    preact = preact + cross_bias.astype(jnp.float32)[None, :]
    base_grad = (out_grad.astype(jnp.float32) * preact).astype(jnp.bfloat16)
    rows = hidden_panel
    branch = lax.psum_scatter(
        jnp.dot(rows, cross_weight, preferred_element_type=jnp.float32).astype(jnp.bfloat16),
        "row",
        scatter_dimension=0,
        tiled=True,
    )
    return (weight_grad, bias_grad, base_grad, branch)


def solution(mesh):
    in_specs = (P("col", "row"), P("row", "col"), P("col", "row"), P("row", "col"), P("row"))
    out_specs = (P("row", "col"), P("row"), P("col", "row"), P("row", "col"))
    return jax.shard_map(
        on_device, mesh=mesh, in_specs=in_specs, out_specs=out_specs, check_vma=False
    )
```

profile of v0, /device:TPU:16, one launch (start us, length us, event | category | flops | bytes accessed | tf_op | source)
XLA Modules:
  0.0 573.2 jit_solution(8535226228451038034)
XLA Ops:
  7.2 0.0 copy-start
  7.2 0.0 all-gather.8.cloned.1.call-start
  7.2 0.7 all-gather.8.cloned.1.call-update
  7.9 0.0 all-gather.6.cloned.1.call-start
  8.0 0.7 all-gather.6.cloned.1.call-update
  8.7 0.0 all-gather.4.cloned.1.call-start
  8.7 0.7 all-gather.4.cloned.1.call-update
  9.4 0.0 reduce-scatter.3.cloned.1.call-start
  9.4 89.4 %all-gather.8.cloned.1.call-done = bf16[1024,512]{1,0:T(8,128)(2,1)} async-done(((bf16[64,512]{1,0:T(8,128)(2,1)}), bf16[1024,512]{1,0:T(8,128)(2,1)}) %all-gather.8.cloned.1.call-update) | async-done | bytes 1048592 | tf_op jit(solution)/shard_map/all_gather | solution.py:8
  98.9 0.0 copy-done
  98.9 3.8 convolution_convert_fusion
  102.7 0.0 reduce-scatter.3.cloned.1.call-update
  102.7 0.0 copy-start.4
  102.7 0.0 reduce-scatter.5.cloned.1.call-start
  102.8 63.9 %all-gather.6.cloned.1.call-done = bf16[1024,1024]{1,0:T(8,128)(2,1)} async-done(((bf16[32,1024]{1,0:T(8,128)(2,1)}), bf16[1024,1024]{1,0:T(8,128)(2,1)}) %all-gather.6.cloned.1.call-update) | async-done | bytes 2097168 | tf_op jit(solution)/shard_map/all_gather | solution.py:11
  166.7 69.4 %all-gather.4.cloned.1.call-done = bf16[1024,1024]{1,0:T(8,128)(2,1)} async-done(((bf16[32,1024]{1,0:T(8,128)(2,1)}), bf16[1024,1024]{1,0:T(8,128)(2,1)}) %all-gather.4.cloned.1.call-update) | async-done | bytes 2097168 | tf_op jit(solution)/shard_map/all_gather | solution.py:10
  236.0 0.0 copy-start.1
  236.0 4.6 convolution_convert_fusion.1
  240.7 0.0 reduce-scatter.5.cloned.1.call-update
  240.7 0.0 copy-done.4
  240.7 0.0 copy-done.1
  240.7 0.0 copy-start.2
  240.7 0.0 copy-start.5
  240.8 3.3 convert_reduce_fusion
  244.1 0.0 copy-done.2
  244.1 0.0 copy-done.5
  244.1 0.0 copy-start.3
  244.1 2.6 fusion
  246.7 113.2 %reduce-scatter.3.cloned.1.call-done = bf16[32,1024]{1,0:T(8,128)(2,1)} async-done(((bf16[1024,1024]{1,0:T(8,128)(2,1)}), bf16[32,1024]{1,0:T(8,128)(2,1)}) %reduce-scatter.3.cloned.1.call-update) | async-done | bytes 65552 | tf_op jit(solution)/shard_map/reduce_scatter | solution.py:21
  359.9 0.0 copy-done.3
  359.9 1.5 multiply_convert_fusion.1
  361.4 205.3 %reduce-scatter.5.cloned.1.call-done = bf16[64,512]{1,0:T(8,128)(2,1)} async-done(((bf16[1024,512]{1,0:T(8,128)(2,1)}), bf16[64,512]{1,0:T(8,128)(2,1)}) %reduce-scatter.5.cloned.1.call-update) | async-done | bytes 65552 | tf_op jit(solution)/shard_map/reduce_scatter | solution.py:32
  (1 shorter events, 0.0 us)
Async XLA Ops:
  7.2 91.7 %copy-start = (bf16[1024,512]{1,0:T(8,128)(2,1)S(1)}, bf16[1024,512]{1,0:T(8,128)(2,1)}, u32[]{:S(2)}) copy-start(bf16[1024,512]{1,0:T(8,128)(2,1)} %param.8) | copy-start | bytes 3145732
  7.2 91.7 %all-gather.8.cloned.1.call-start = ((), (), s32[]{:S(2)}) async-start(), calls=%async_computation.4 | async-start | bytes 1114112 | tf_op jit(solution)/shard_map/all_gather | solution.py:8
  7.9 158.7 %all-gather.6.cloned.1.call-start = ((), (), s32[]{:S(2)}) async-start(), calls=%async_computation.3 | async-start | bytes 2162688 | tf_op jit(solution)/shard_map/all_gather | solution.py:11
  8.7 227.4 %all-gather.4.cloned.1.call-start = ((), (), s32[]{:S(2)}) async-start(), calls=%async_computation.2 | async-start | bytes 2162688 | tf_op jit(solution)/shard_map/all_gather | solution.py:10
  9.4 350.5 %reduce-scatter.3.cloned.1.call-start = ((), (), s32[]{:S(2)}) async-start(), calls=%async_computation.5 | async-start | bytes 2162688 | tf_op jit(solution)/shard_map/reduce_scatter | solution.py:21
  102.7 138.0 %copy-start.4 = (bf16[1024]{0:T(1024)(128)(2,1)S(1)}, bf16[1024]{0:T(1024)(128)(2,1)}, u32[]{:S(2)}) copy-start(bf16[1024]{0:T(1024)(128)(2,1)} %param.9) | copy-start | bytes 6148
  102.7 463.9 %reduce-scatter.5.cloned.1.call-start = ((), (), s32[]{:S(2)}) async-start(), calls=%async_computation.6 | async-start | bytes 1114112 | tf_op jit(solution)/shard_map/reduce_scatter | solution.py:32
  236.0 4.7 copy-start.1
  240.7 3.3 copy-start.2
  240.7 3.3 copy-start.5
  244.1 115.8 %copy-start.3 = (bf16[32,1024]{1,0:T(8,128)(2,1)S(1)}, bf16[32,1024]{1,0:T(8,128)(2,1)}, u32[]{:S(2)}) copy-start(bf16[32,1024]{1,0:T(8,128)(2,1)} %param.7) | copy-start | bytes 196612
Sparse Core Ops, SparseCore 0:
  11.2 87.6 all-gather.7
  101.0 65.6 all-gather.5
  168.8 67.1 all-gather.3
  238.7 121.1 reduce-scatter.2
  365.4 201.2 reduce-scatter.4
where the time goes:
time: 573 us
  waiting for transfers between devices  543 us (95%)
  between operations  13.8 us (2%)
  matrix products  11.1 us (2%)
    reduce_scatter x1, waiting for transfers between devices, on_device(): lax.psum_scatter(jnp.dot(rows, cross_weight, preferred_element_type=jnp.f...  205 us
    reduce_scatter x1, waiting for transfers between devices, on_device(): lax.psum_scatter(lax.dot_general(rows, cross_weight, (((1,), (1,)), ((),...  113 us
    all_gather x1, waiting for transfers between devices, on_device(): input_panel = lax.all_gather(layer_input, 'row', axis=0, tiled=True)  89.4 us
    all_gather x1, waiting for transfers between devices, on_device(): lax.all_gather(out_grad, 'col', axis=0, tiled=True)  69.4 us
    all_gather x1, waiting for transfers between devices, on_device(): lax.all_gather(base_input, 'col', axis=0, tiled=True)  63.9 us
  transfers between devices with their start and end apart: 5, of which 5 were waited for; matrix products, arithmetic and copies ran while one was open for 3% of the time, Pallas kernels for 0%

commit v1 on v0

--- a/solution.py
+++ b/solution.py
@@ -2,13 +2,21 @@
 import jax.numpy as jnp
 from jax import lax
 from jax.sharding import PartitionSpec as P
+from jax.lax import all_to_all, axis_size
 
 
 def on_device(base_input, layer_input, out_grad, cross_weight, cross_bias):
     input_panel = lax.all_gather(layer_input, "row", axis=0, tiled=True)
+
+    def lots_all_lay(x_local):
+        plain = tuple((x_local for _ in range(axis_size("col"))))
+        side_arr = jnp.stack(plain)
+        aux = all_to_all(side_arr, "col", 0, 0)
+        return jnp.concatenate(aux, axis=0)
+
     grad_panel, base_panel = (
         lax.all_gather(out_grad, "col", axis=0, tiled=True),
-        lax.all_gather(base_input, "col", axis=0, tiled=True),
+        lots_all_lay(base_input),
     )
     hidden_panel = (grad_panel.astype(jnp.float32) * base_panel.astype(jnp.float32)).astype(
         jnp.bfloat16

time: 573 us -> 505 us (0.88)
  waiting for transfers between devices: 543 us -> 460 us
  starting transfers between devices: 0.19 us -> 11.8 us
    all_gather x1 -> x0, waiting for transfers between devices: 63.9 us -> none  [on_device(): lax.all_gather(base_input, 'col', axis=0, tiled=True)]
    all_gather x1, waiting for transfers between devices: 89.4 us -> 76.3 us  [on_device(): input_panel = lax.all_gather(layer_input, 'row', axis=0, tiled=True)]
    all_to_all x0 -> x1, starting transfers between devices: none -> 11.6 us  [lots_all_lay(): aux = all_to_all(side_arr, 'col', 0, 0)]
  transfers between devices with their start and end apart: 5 -> 5, of which waited for: 5 -> 4; matrix products, arithmetic and copies ran while one was open for 3% -> 3% of each run, Pallas kernels for 0% -> 0%
where the time goes in v1:
time: 505 us; the launch traced here: 504 us
  waiting for transfers between devices  460 us (91%)
  between operations  13.8 us (3%)
  starting transfers between devices  11.8 us (2%)
  matrix products  10.3 us (2%)
    reduce_scatter x1, waiting for transfers between devices, on_device(): lax.psum_scatter(jnp.dot(rows, cross_weight, preferred_element_type=jnp.f...  205 us
    reduce_scatter x1, waiting for transfers between devices, on_device(): lax.psum_scatter(lax.dot_general(rows, cross_weight, (((1,), (1,)), ((),...  113 us
    all_gather x1, waiting for transfers between devices, on_device(): input_panel = lax.all_gather(layer_input, 'row', axis=0, tiled=True)  76.3 us
    all_gather x1, waiting for transfers between devices, on_device(): lax.all_gather(out_grad, 'col', axis=0, tiled=True)  63.9 us
    all_to_all x1, starting transfers between devices, lots_all_lay(): aux = all_to_all(side_arr, 'col', 0, 0)  11.6 us
  transfers between devices with their start and end apart: 5, of which 4 were waited for; matrix products, arithmetic and copies ran while one was open for 3% of the time, Pallas kernels for 0%

profile of v1, /device:TPU:16, one launch (start us, length us, event | category | flops | bytes accessed | tf_op | source)
XLA Modules:
  0.0 504.3 jit_solution(2644778537750879070)
XLA Ops:
  7.2 0.0 copy-start
  7.2 0.0 all-gather.5.cloned.1.call-start
  7.2 0.7 all-gather.5.cloned.1.call-update
  7.9 0.0 all-gather.3.cloned.1.call-start
  8.0 0.7 all-gather.3.cloned.1.call-update
  8.7 2.4 stack.2
  11.1 11.6 %all-to-all-start = ((bf16[32,32,1024]{2,1,0:T(8,128)(2,1)}), bf16[32,32,1024]{2,1,0:T(8,128)(2,1)S(1)}, u32[]{:S(2)}, u32[]{:S(2)}) async-start(bf16[32,32,1024]{2,1,0:T(8,128)(2,1)} %stack.2), calls=%async_computation | async-start | bytes 4194304 | tf_op jit(solution)/shard_map/all_to_all | solution.py:14
  22.7 0.0 reduce-scatter.3.cloned.1.call-start
  22.8 76.3 %all-gather.5.cloned.1.call-done = bf16[1024,512]{1,0:T(8,128)(2,1)} async-done(((bf16[64,512]{1,0:T(8,128)(2,1)}), bf16[1024,512]{1,0:T(8,128)(2,1)}) %all-gather.5.cloned.1.call-update) | async-done | bytes 1048592 | tf_op jit(solution)/shard_map/all_gather | solution.py:9
  99.1 0.0 copy-done
  99.1 3.8 convolution_convert_fusion
  102.9 0.0 reduce-scatter.3.cloned.1.call-update
  103.0 0.0 reduce-scatter.5.cloned.1.call-start
  103.0 0.0 all-to-all-done
  103.0 63.9 %all-gather.3.cloned.1.call-done = bf16[1024,1024]{1,0:T(8,128)(2,1)} async-done(((bf16[32,1024]{1,0:T(8,128)(2,1)}), bf16[1024,1024]{1,0:T(8,128)(2,1)}) %all-gather.3.cloned.1.call-update) | async-done | bytes 2097168 | tf_op jit(solution)/shard_map/all_gather | solution.py:18
  166.9 3.4 convert_reduce_fusion
  170.3 0.0 copy-start.1
  170.3 1.3 copy-done.1
  171.6 0.0 copy-start.3
  171.6 0.0 copy-start.4
  171.6 2.2 convolution_convert_fusion.1
  173.8 0.0 reduce-scatter.5.cloned.1.call-update
  173.8 0.0 copy-done.3
  173.9 0.0 copy-done.4
  173.9 0.0 copy-start.2
  173.9 4.2 fusion.2
  178.1 112.8 %reduce-scatter.3.cloned.1.call-done = bf16[32,1024]{1,0:T(8,128)(2,1)} async-done(((bf16[1024,1024]{1,0:T(8,128)(2,1)}), bf16[32,1024]{1,0:T(8,128)(2,1)}) %reduce-scatter.3.cloned.1.call-update) | async-done | bytes 65552 | tf_op jit(solution)/shard_map/reduce_scatter | solution.py:29
  290.9 0.0 copy-done.2
  290.9 1.5 multiply_convert_fusion
  292.4 205.3 %reduce-scatter.5.cloned.1.call-done = bf16[64,512]{1,0:T(8,128)(2,1)} async-done(((bf16[1024,512]{1,0:T(8,128)(2,1)}), bf16[64,512]{1,0:T(8,128)(2,1)}) %reduce-scatter.5.cloned.1.call-update) | async-done | bytes 65552 | tf_op jit(solution)/shard_map/reduce_scatter | solution.py:40
  (1 shorter events, 0.0 us)
Async XLA Ops:
  7.2 91.9 %copy-start = (bf16[1024,512]{1,0:T(8,128)(2,1)S(1)}, bf16[1024,512]{1,0:T(8,128)(2,1)}, u32[]{:S(2)}) copy-start(bf16[1024,512]{1,0:T(8,128)(2,1)} %param.8) | copy-start | bytes 3145732
  7.2 91.9 %all-gather.5.cloned.1.call-start = ((), (), s32[]{:S(2)}) async-start(), calls=%async_computation.4 | async-start | bytes 1114112 | tf_op jit(solution)/shard_map/all_gather | solution.py:9
  7.9 159.0 %all-gather.3.cloned.1.call-start = ((), (), s32[]{:S(2)}) async-start(), calls=%async_computation.3 | async-start | bytes 2162688 | tf_op jit(solution)/shard_map/all_gather | solution.py:18
  11.1 91.9 %all-to-all-start = ((bf16[32,32,1024]{2,1,0:T(8,128)(2,1)}), bf16[32,32,1024]{2,1,0:T(8,128)(2,1)S(1)}, u32[]{:S(2)}, u32[]{:S(2)}) async-start(bf16[32,32,1024]{2,1,0:T(8,128)(2,1)} %stack.2), calls=%async_computation | async-start | bytes 4194304 | tf_op jit(solution)/shard_map/all_to_all | solution.py:14
  22.7 268.2 %reduce-scatter.3.cloned.1.call-start = ((), (), s32[]{:S(2)}) async-start(), calls=%async_computation.5 | async-start | bytes 2162688 | tf_op jit(solution)/shard_map/reduce_scatter | solution.py:29
  103.0 394.8 %reduce-scatter.5.cloned.1.call-start = ((), (), s32[]{:S(2)}) async-start(), calls=%async_computation.6 | async-start | bytes 1114112 | tf_op jit(solution)/shard_map/reduce_scatter | solution.py:40
  170.3 1.3 copy-start.1
  171.6 2.3 copy-start.3
  171.6 2.3 copy-start.4
  173.9 117.0 %copy-start.2 = (bf16[32,1024]{1,0:T(8,128)(2,1)S(1)}, bf16[32,1024]{1,0:T(8,128)(2,1)}, u32[]{:S(2)}) copy-start(bf16[32,1024]{1,0:T(8,128)(2,1)} %param.7) | copy-start | bytes 196612
Sparse Core Ops, SparseCore 0:
  11.2 87.8 all-gather.4
  101.3 65.6 all-gather.2
  169.7 121.1 reduce-scatter.2
  296.4 201.3 reduce-scatter.4
